TPU v7x, 32 devices: a whole 2x2x4 slice. The times are simulated.
32 devices in a mesh: groups: 2 (over x), date: 16 (over z, y, core).
Axes of the slice: x: 2, y: 2, z: 4, core: 2. Of those that a mesh axis runs over, the one named last changes fastest.
Arguments:
- images: float32 [32, 2, 64, 2560], P(('groups', 'date')), parts along dimension 0, may hold values from -16 to 16
- height_phase: float32 [128, 2560], P(('groups', 'date')), parts along dimension 0, may hold values from -4 to 4
- baseline: float32 [32], P('groups'), parts along dimension 0, may hold values from -0.6 to 0.6
- pair_list: int32 [32, 2], replicated, may hold values from 0 to 15, as said below
- pair_owner: int32 [32, 1], replicated, may hold values from 0 to 15; in each aligned block of 32 rows (0 to 31, 32 to 63, ...) at most 4 rows name the same one
Outputs:
- interferogram: float32 [128, 2, 16, 128], P(('groups', 'date')), parts along dimension 0
- coherence: float32 [128, 16, 128], P(('groups', 'date')), parts along dimension 0
There are 2 independent parts, one for each index of `groups`. A program takes and returns all parts, laid end to end along the dimension named above; an argument that names none is the same for every part. Nothing has to cross between parts.
Inputs may be any that keep to these rules, and one draw needn't show every extreme that they name: `pair_list`: each row is (r, s) with r < s <= r + 4; some pair has s = r + 4. `pair_owner`: every index owns at least one pair and at most 4 pairs; some index owns exactly 4.
All inputs are finite; a program needn't handle non-finite values.
Results may differ from a plain program's by a relative error of at most 0.00007.
Values sent between devices are 32-bit elements; how exact they have to be, the bound alone decides.
A program may use at most 128 MiB of HBM per device.

v0:
```python
import jax
import jax.numpy as jnp
from jax import lax
from jax.sharding import PartitionSpec as P

LOOK_ROWS = 4
LOOK_COLS = 20
CAP = 4


EPSILON = 1e-06


def box_matrix(columns):
    position = jnp.arange(columns, dtype=jnp.int32)
    target = jnp.arange(columns // LOOK_COLS, dtype=jnp.int32)
    return (position[:, None] // LOOK_COLS == target[None, :]).astype(jnp.float32)


def multilook(values):
    values_shape = values.shape
    row_count = values_shape[-2]
    columns = values_shape[-1]
    summed = jnp.sum(
        values.reshape(values_shape[:-2] + (row_count // LOOK_ROWS, LOOK_ROWS, columns)), axis=-2
    )
    flattened = summed.reshape(-1, columns)
    looked = jnp.dot(
        flattened,
        box_matrix(columns),
        precision=lax.Precision.HIGHEST,
        preferred_element_type=jnp.float32,
    )
    return looked.reshape(values_shape[:-2] + (row_count // LOOK_ROWS, columns // LOOK_COLS)) / (
        LOOK_ROWS * LOOK_COLS
    )


def flatten_phase(images, factors, height_phase):
    phase_angle = factors[:, None, None] * height_phase[None]
    cosine = jnp.cos(phase_angle)
    sine_part = jnp.sin(phase_angle)
    real_part = images[:, 0] * cosine - images[:, 1] * sine_part
    imag_part = images[:, 0] * sine_part + images[:, 1] * cosine
    return (real_part, imag_part)


def pair_terms(first_real, first_imag, second_real, second_imag, first_power, second_power):
    look_real = multilook(first_real * second_real + first_imag * second_imag)
    look_imag = multilook(first_imag * second_real - first_real * second_imag)
    denominator = jnp.sqrt((first_power + EPSILON) * (second_power + EPSILON))
    coherence = jnp.sqrt(look_real * look_real + look_imag * look_imag) / denominator
    return jnp.stack([look_real, look_imag, coherence], axis=-3)


def body(images, height_phase, baseline, pair_list, pair_owner):
    devices = lax.axis_size("date")
    owners = pair_owner[:, 0]
    first_index = pair_list[:, 0]
    second_index = pair_list[:, 1]
    gathered = lax.all_to_all(images, "date", split_axis=2, concat_axis=0, tiled=True)
    real_part, imag_part = flatten_phase(gathered, baseline, height_phase)
    power_map = multilook(real_part * real_part + imag_part * imag_part)
    quantities = pair_terms(
        real_part[first_index],
        imag_part[first_index],
        real_part[second_index],
        imag_part[second_index],
        power_map[first_index],
        power_map[second_index],
    )
    source = jnp.arange(pair_list.shape[0], dtype=jnp.int32)
    position = jnp.arange(owners.shape[0], dtype=jnp.int32)
    earlier = (owners[:, None] == owners[None, :]) & (position[:, None] > position[None, :])
    slot_index = owners * CAP + jnp.sum(earlier.astype(jnp.int32), axis=1)
    slot_count = CAP * devices
    slot_range = jnp.arange(slot_count, dtype=jnp.int32)
    taken = (slot_index[None, :] == slot_range[:, None]).astype(jnp.int32)
    picked = jnp.sum(taken * (source[None, :] + 1), axis=1) - 1
    column_range = jnp.arange(quantities.shape[0], dtype=jnp.int32)
    selector = (picked[:, None] == column_range[None, :]).astype(jnp.float32)
    buffer = jnp.einsum(
        "sq,qkrc->skrc",
        selector,
        quantities,
        precision=lax.Precision.HIGHEST,
        preferred_element_type=jnp.float32,
    )
    delivered = lax.all_to_all(buffer, "date", split_axis=0, concat_axis=2, tiled=True)
    return (delivered[:, :2], delivered[:, 2])


def solution(mesh):
    in_specs = (
        P(("groups", "date"), None, None, None),
        P(("groups", "date"), None),
        P("groups"),
        P(),
        P(),
    )
    out_specs = (P(("groups", "date"), None, None, None), P(("groups", "date"), None, None))
    return jax.shard_map(body, mesh=mesh, in_specs=in_specs, out_specs=out_specs, check_vma=False)
```

profile of v0, /device:TPU:0, one launch (start us, length us, event | category | flops | bytes accessed | tf_op | source)
XLA Modules:
  0.0 79.0 jit_solution(1218121472605938797)
XLA Ops:
  0.6 3.4 %copy.25 = f32[1,2,64,2560]{3,1,0,2:T(2,128)} copy(f32[1,2,64,2560]{3,2,1,0:T(8,128)} %param.5) | data formatting | bytes 2621440 | tf_op args[0]
  4.0 0.0 copy-start.2
  4.0 0.0 copy-start.3
  4.0 7.5 %all-to-all-start = ((f32[1,2,64,2560]{3,1,0,2:T(2,128)}), f32[1,2,64,2560]{3,1,0,2:T(2,128)S(1)}, u32[]{:S(2)}, u32[]{:S(2)}) async-start(f32[1,2,64,2560]{3,1,0,2:T(2,128)} %copy.25), calls=%async_computation | async-start | bytes 2621440 | tf_op jit(solution)/shard_map/all_to_all | solution.py:61
  11.6 0.0 copy-done.2
  11.6 0.0 copy-done.3
  11.6 0.2 convert_reduce_fusion
  11.8 0.1 select_reduce_fusion
  11.9 26.9 %all-to-all-done = f32[1,2,64,2560]{3,1,0,2:T(2,128)S(1)} async-done(((f32[1,2,64,2560]{3,1,0,2:T(2,128)}), f32[1,2,64,2560]{3,1,0,2:T(2,128)S(1)}, u32[]{:S(2)}, u32[]{:S(2)}) %all-to-all-start) | async-done | bytes 1310752 | tf_op jit(solution)/shard_map/all_to_all | solution.py:61
  38.9 0.0 copy-start
  38.9 0.8 copy.36
  39.6 0.0 copy-done
  39.6 0.0 copy-done.1
  39.6 2.9 %fusion.17 = f32[16,2560]{1,0:T(8,128)S(1)} fusion(f32[16,2,4,2560]{3,0,2,1:T(8,128)S(1)} %bitcast.41, f32[4,2560]{1,0:T(4,128)S(1)} %copy-done, f32[16]{0:T(128)S(1)} %copy-done.1), kind=kLoop, calls=%fused_computation.32 | loop fusion | flops 1761280 | bytes 1515584 | tf_op jit(solution)/shard_map/reduce_sum | solution.py:24
  42.5 3.4 %fusion.20 = (f32[16,4,2560]{2,0,1:T(8,128)}, f32[16,4,2560]{2,0,1:T(8,128)S(1)}) fusion(f32[16,2,4,2560]{3,0,2,1:T(8,128)S(1)} %bitcast.42, f32[4,2560]{1,0:T(4,128)S(1)} %copy-done, f32[16]{0:T(128)S(1)} %copy-done.1), kind=kLoop, calls=%fused_computation.35 | loop fusion | flops 1146880 | bytes 2662464 | tf_op jit(solution)/shard_map/sub | solution.py:43
  45.9 0.7 fusion.5
  46.6 0.6 gather_fusion.5
  47.2 0.6 gather_fusion.4
  47.8 0.4 copy.29
  48.2 1.3 %gather_fusion.2 = f32[32,4,2560]{2,1,0:T(4,128)S(1)} fusion(f32[16,4,2560]{2,1,0:T(4,128)S(1)} %copy.29, s32[1024]{0:T(1024)S(1)} %get-tuple-element.21), kind=kCustom, calls=%fused_computation.2 | custom fusion | bytes 2621568 | tf_op jit(solution)/shard_map/gather | solution.py:66
  49.5 1.3 %gather_fusion.3 = f32[32,4,2560]{2,1,0:T(4,128)S(1)} fusion(f32[16,4,2560]{2,1,0:T(4,128)S(1)} %copy.29, s32[1024]{0:T(1024)S(1)} %get-tuple-element.20), kind=kCustom, calls=%fused_computation.3 | custom fusion | bytes 2621568 | tf_op jit(solution)/shard_map/gather | solution.py:68
  50.9 1.5 %copy.27 = f32[16,4,2560]{2,1,0:T(4,128)S(1)} copy(f32[16,4,2560]{2,0,1:T(8,128)} %get-tuple-element.16) | data formatting | bytes 1310720 | tf_op jit(solution)/shard_map/sub | solution.py:43
  52.4 2.3 %gather_fusion = f32[32,4,2560]{2,1,0:T(4,128)} fusion(f32[16,4,2560]{2,1,0:T(4,128)S(1)} %copy.27, s32[1024]{0:T(1024)S(1)} %get-tuple-element.21), kind=kCustom, calls=%fused_computation | custom fusion | bytes 2621568 | tf_op jit(solution)/shard_map/gather | solution.py:65
  54.7 2.3 %gather_fusion.1 = f32[32,4,2560]{2,1,0:T(4,128)} fusion(f32[16,4,2560]{2,1,0:T(4,128)S(1)} %copy.27, s32[1024]{0:T(1024)S(1)} %get-tuple-element.20), kind=kCustom, calls=%fused_computation.1 | custom fusion | bytes 2621568 | tf_op jit(solution)/shard_map/gather | solution.py:67
  57.0 3.6 %add_reduce_fusion = (f32[32,2560]{1,0:T(8,128)S(1)}, f32[32,2560]{1,0:T(8,128)S(1)}) fusion(f32[32,4,2560]{2,1,0:T(4,128)S(1)} %gather_fusion.2, f32[32,4,2560]{2,1,0:T(4,128)S(1)} %gather_fusion.3, f32[32,4,2560]{2,1,0:T(4,128)} %gather_fusion, f32[32,4,2560]{2,1,0:T(4,128)} %gather_fusion.1), kind=kLoop, calls=%fused_computation.12 | loop fusion | flops 2457600 | bytes 5898240 | tf_op jit(solution)/shard_map/reduce_sum | solution.py:24
  60.7 0.7 fusion.4
  61.4 0.7 fusion.3
  62.1 0.2 convolution_bitcast_fusion
  62.4 0.1 copy.31
  62.5 15.2 %all_to_all.36 = f32[64,3,1,128]{3,2,1,0:T(1,128)S(1)} all-to-all(f32[64,3,1,128]{3,2,1,0:T(1,128)S(1)} %copy.31), channel_id=1, replica_groups=mesh['groups'=2,'date'=16] {'date'}, dimensions={0} | all-to-all | bytes 196608 | tf_op jit(solution)/shard_map/all_to_all | solution.py:89
  77.7 0.6 slice_bitcast_fusion
  78.3 0.6 copy.33
  (9 shorter events, 0.1 us)
Async XLA Ops:
  4.0 7.6 %copy-start.2 = (s32[32,2]{0,1:T(2,128)S(1)}, s32[32,2]{0,1:T(2,128)}, u32[]{:S(2)}) copy-start(s32[32,2]{0,1:T(2,128)} %param.8) | copy-start | bytes 772
  4.0 7.6 %copy-start.3 = (s32[32,1]{0,1:T(1,128)S(1)}, s32[32,1]{0,1:T(1,128)}, u32[]{:S(2)}) copy-start(s32[32,1]{0,1:T(1,128)} %param.9) | copy-start | bytes 388
  4.0 34.8 %all-to-all-start = ((f32[1,2,64,2560]{3,1,0,2:T(2,128)}), f32[1,2,64,2560]{3,1,0,2:T(2,128)S(1)}, u32[]{:S(2)}, u32[]{:S(2)}) async-start(f32[1,2,64,2560]{3,1,0,2:T(2,128)} %copy.25), calls=%async_computation | async-start | bytes 2621440 | tf_op jit(solution)/shard_map/all_to_all | solution.py:61
  38.9 0.8 copy-start
  38.9 0.8 copy-start.1
where the time goes:
time: 79.4 us; the launch traced here: 79 us
  waiting for transfers between devices  26.9 us (34%)
  local copies, waits for them, and re-layouts  15.9 us (20%)
  blocking collectives  15.2 us (19%)
  other arithmetic  10.3 us (13%)
  starting transfers between devices  7.55 us (10%)
  matrix products  2.33 us (3%)
    all_to_all x1, waiting for transfers between devices, body(): lax.all_to_all(images, 'date', split_axis=2, concat_axis=0, tiled=True)  26.9 us
    all_to_all x1, blocking collectives, body(): lax.all_to_all(buffer, 'date', split_axis=0, concat_axis=2, tiled=True)  15.2 us
    all_to_all x1, starting transfers between devices, body(): lax.all_to_all(images, 'date', split_axis=2, concat_axis=0, tiled=True)  7.55 us
    reduce_sum x2, other arithmetic, multilook(): jnp.sum(values.reshape(values_shape[:-2] + (row_count // LOOK_ROWS, LOOK_...  6.5 us
    unnamed x10, local copies, waits for them, and re-layouts  4.05 us
    sub x1, other arithmetic, flatten_phase(): real_part = images[:, 0] * cosine - images[:, 1] * sine_part  3.42 us
    gather x1, local copies, waits for them, and re-layouts, body(): real_part[second_index]  2.33 us
    gather x1, local copies, waits for them, and re-layouts, body(): real_part[first_index]  2.31 us
  transfers between devices with their start and end apart: 1, of which 1 were waited for; matrix products, arithmetic and copies ran while one was open for 0% of the time, Pallas kernels for 0%

commit v1 on v0

v1 whole, which is shorter than its diff:
```python
import functools

import jax
import jax.numpy as jnp
from jax import lax
from jax.experimental import pallas as pl
from jax.experimental.pallas import tpu as pltpu
from jax.sharding import PartitionSpec as P

LOOK_ROWS = 4
LOOK_COLS = 20
CAP = 4
BAND = 4
EPSILON = 1e-06
LANES = 128
TILE = 8
GROUP = 16


def split(values, parts):
    pieces = []
    for _ in range(parts):
        piece = values.astype(jnp.bfloat16)
        pieces.append(piece)
        values = values - piece.astype(jnp.float32)
    return pieces


def kernel(
    devices, chunks, images, height, baseline, pair_list, pair_owner, looks_out, coherence_out,
    recv, heights, cosines, sines, box, sums, pick_look, pick_first, pick_second,
    stack_real, stack_imag, stack_power, outbox, inbox,
    send_sem, recv_sem, own_sem, height_sem, out_send_sem, out_recv_sem,
):
    me = lax.axis_index("date")
    half = images.shape[2] // 2
    width = half // chunks
    core = lax.rem(me, 2)
    partner = me + 1 - 2 * core

    def peer(step):
        return lax.rem(me + step, devices)

    barrier = pltpu.get_barrier_semaphore()

    @pl.loop(1, devices)
    def _(step):
        pl.semaphore_signal(barrier, inc=1, device_id={"date": peer(step)})

    pl.semaphore_wait(barrier, devices - 1)

    def lines(target, chunk):
        first = pl.multiple_of(lax.div(target, 2) * TILE, TILE)
        column = pl.multiple_of(lax.rem(target, 2) * half + chunk * width, LANES)
        return images.at[:, pl.ds(first, TILE), pl.ds(column, width)]

    def landing(source, chunk):
        return recv.at[chunk, :, pl.ds(pl.multiple_of(source * TILE, TILE), TILE), :]

    def line_copy(target, chunk):
        return pltpu.make_async_remote_copy(
            src_ref=lines(target, chunk),
            dst_ref=landing(me, chunk),
            send_sem=send_sem.at[chunk, target],
            recv_sem=recv_sem.at[chunk, me],
            device_id={"date": target},
        )

    def line_arrival(source, chunk):
        return pltpu.make_async_remote_copy(
            src_ref=lines(source, chunk),
            dst_ref=landing(source, chunk),
            send_sem=send_sem.at[chunk, source],
            recv_sem=recv_sem.at[chunk, source],
            device_id={"date": source},
        )

    def own_copy(chunk):
        return pltpu.make_async_copy(lines(me, chunk), landing(me, chunk), own_sem.at[chunk])

    def columns_of(which):
        return height.at[:, pl.ds(pl.multiple_of(which * half, LANES), half)]

    height_own = pltpu.make_async_copy(columns_of(core), heights.at[core], height_sem.at[0])
    height_away = pltpu.make_async_remote_copy(
        src_ref=columns_of(1 - core),
        dst_ref=heights.at[core],
        send_sem=height_sem.at[1],
        recv_sem=height_sem.at[2],
        device_id={"date": partner},
    )
    height_own.start()
    height_away.start()

    @pl.loop(0, chunks)
    def _(chunk):
        @pl.loop(1, devices)
        def _(step):
            line_copy(peer(step), chunk).start()

        own_copy(chunk).start()

    rows = box.shape[0]
    position = lax.broadcasted_iota(jnp.int32, (rows, LANES), 0)
    target = lax.broadcasted_iota(jnp.int32, (rows, LANES), 1) * LOOK_COLS
    box[...] = jnp.where(
        (position >= target) & (position < target + LOOK_COLS), 1.0, 0.0
    ).astype(jnp.bfloat16)

    def as_column(row):
        size = row.shape[1]
        down = lax.broadcasted_iota(jnp.int32, (size, size), 0)
        across = lax.broadcasted_iota(jnp.int32, (size, size), 1)
        return jnp.sum(
            jnp.where(down == across, jnp.broadcast_to(row, (size, size)), 0.0), axis=1, keepdims=True
        )

    owner = pair_owner[...].astype(jnp.float32)
    pairs = owner.shape[1]
    down = lax.broadcasted_iota(jnp.int32, (pairs, pairs), 0)
    across = lax.broadcasted_iota(jnp.int32, (pairs, pairs), 1)
    earlier = (as_column(owner) == owner) & (down < across)
    place = owner * GROUP + jnp.sum(jnp.where(earlier, 1.0, 0.0), axis=0, keepdims=True)
    first = pair_list[0:1, :].astype(jnp.float32)
    second = pair_list[1:2, :].astype(jnp.float32)
    band = (second - first - 1.0) * devices + first
    total = devices * GROUP
    line = lax.broadcasted_iota(jnp.int32, (total, pairs), 0)
    line = (line - (line & 12)).astype(jnp.float32)
    taken = line == place

    def listed(value):
        return jnp.sum(jnp.where(taken, value + 1.0, 0.0), axis=1, keepdims=True) - 1.0

    def one_hot(value, size):
        lane = lax.broadcasted_iota(jnp.int32, (total, 3 * size), 1) & (size - 1)
        return jnp.where(lane.astype(jnp.float32) == value, 1.0, 0.0).astype(jnp.bfloat16)

    pick_look[...] = one_hot(listed(band), BAND * devices)
    pick_first[...] = one_hot(listed(first), devices)
    pick_second[...] = one_hot(listed(second), devices)
    scale = as_column(baseline[...])
    sums[...] = jnp.zeros_like(sums)

    height_own.wait()
    height_away.wait()

    for row in range(TILE):
        @pl.loop(0, half // LANES)
        def _(block):
            column = pl.ds(pl.multiple_of(block * LANES, LANES), LANES)
            level = heights[row // LOOK_ROWS, row % LOOK_ROWS:row % LOOK_ROWS + 1, column]
            angle = scale * level
            cosines[row, :, column] = jnp.cos(angle)
            sines[row, :, column] = jnp.sin(angle)

    @pl.loop(0, chunks)
    def _(chunk):
        own_copy(chunk).wait()

        @pl.loop(1, devices)
        def _(step):
            line_arrival(peer(step), chunk).wait_recv()

        column = pl.multiple_of(chunk * width, width)
        outer = pl.ds(column, width)
        summed = sums[...]
        for look_row in range(TILE // LOOK_ROWS):
            totals = [None] * (1 + 2 * BAND)

            def add(at, value):
                totals[at] = value if totals[at] is None else totals[at] + value

            for row in range(look_row * LOOK_ROWS, (look_row + 1) * LOOK_ROWS):
                real = recv[chunk, 0, pl.ds(row, devices, stride=TILE), :]
                imag = recv[chunk, 1, pl.ds(row, devices, stride=TILE), :]
                cosine = cosines[row, :, outer]
                sine = sines[row, :, outer]
                flat_real = real * cosine - imag * sine
                flat_imag = real * sine + imag * cosine
                add(0, flat_real * flat_real + flat_imag * flat_imag)
                for distance in range(1, BAND + 1):
                    next_real = pltpu.roll(flat_real, devices - distance, 0)
                    next_imag = pltpu.roll(flat_imag, devices - distance, 0)
                    add(distance, flat_real * next_real + flat_imag * next_imag)
                    add(BAND + distance, flat_imag * next_real - flat_real * next_imag)
            weights = box[pl.ds(pl.multiple_of(look_row * half + column, width), width), :]
            pieces = split(jnp.concatenate(totals, axis=0), 2)
            for piece in pieces:
                summed = summed + jnp.dot(piece, weights, preferred_element_type=jnp.float32)
        sums[...] = summed

    mean = sums[...] * (1.0 / (LOOK_ROWS * LOOK_COLS))
    ends = (0, devices, (1 + BAND) * devices, (1 + 2 * BAND) * devices)
    for stack, low, high in zip((stack_power, stack_real, stack_imag), ends[:-1], ends[1:]):
        for part, piece in enumerate(split(mean[low:high], 3)):
            stack[part * (high - low):(part + 1) * (high - low), :] = piece

    def chosen(pick, stack):
        return jnp.dot(pick[...], stack[...], preferred_element_type=jnp.float32)

    look_real = chosen(pick_look, stack_real)
    look_imag = chosen(pick_look, stack_imag)
    denominator = jnp.sqrt(
        (chosen(pick_first, stack_power) + EPSILON) * (chosen(pick_second, stack_power) + EPSILON)
    )
    ratio = jnp.sqrt(look_real * look_real + look_imag * look_imag) / denominator
    kind = lax.broadcasted_iota(jnp.int32, (total, LANES), 0) & 12
    outbox[...] = jnp.where(kind == 0, look_real, jnp.where(kind == 4, look_imag, ratio))

    def parcel(which):
        return pl.ds(pl.multiple_of(which * GROUP, GROUP), GROUP)

    def out_copy(target):
        return pltpu.make_async_remote_copy(
            src_ref=outbox.at[parcel(target), :],
            dst_ref=inbox.at[parcel(me), :],
            send_sem=out_send_sem.at[target],
            recv_sem=out_recv_sem.at[me],
            device_id={"date": target},
        )

    def out_arrival(source):
        return pltpu.make_async_remote_copy(
            src_ref=outbox.at[parcel(source), :],
            dst_ref=inbox.at[parcel(source), :],
            send_sem=out_send_sem.at[source],
            recv_sem=out_recv_sem.at[source],
            device_id={"date": source},
        )

    @pl.loop(1, devices)
    def _(step):
        out_copy(peer(step)).start()

    inbox[parcel(me), :] = outbox[parcel(me), :]

    @pl.loop(0, chunks)
    def _(chunk):
        @pl.loop(1, devices)
        def _(step):
            line_copy(peer(step), chunk).wait_send()

    @pl.loop(1, devices)
    def _(step):
        out_arrival(peer(step)).wait_recv()

    left = lax.broadcasted_iota(jnp.int32, (devices // 2, LANES), 1) < LANES // 2
    for kind_at in range(3):
        for slot in range(CAP):
            at = kind_at * CAP + slot
            even = inbox[pl.ds(at, devices // 2, stride=2 * GROUP), :]
            odd = inbox[pl.ds(GROUP + at, devices // 2, stride=2 * GROUP), :]
            upper = jnp.where(left, even, pltpu.roll(odd, LANES // 2, 1))
            lower = jnp.where(left, pltpu.roll(even, LANES // 2, 1), odd)
            for look_row, value in enumerate((upper, lower)):
                lines_at = pl.ds(look_row, devices // 2, stride=2)
                if kind_at < 2:
                    looks_out[slot, kind_at, lines_at, :] = value
                else:
                    coherence_out[slot, lines_at, :] = value

    @pl.loop(1, devices)
    def _(step):
        out_copy(peer(step)).wait_send()


def body(images, height_phase, baseline, pair_list, pair_owner):
    devices = lax.axis_size("date")
    rows, columns = images.shape[2:]
    half = columns // 2
    width = LANES
    chunks = half // width
    lanes = columns // LOOK_COLS
    assert lanes == LANES and rows == LOOK_ROWS * devices and half % LANES == 0
    quantities = 1 + 2 * BAND
    total = devices * GROUP
    vmem = pl.BlockSpec(memory_space=pltpu.VMEM)
    anywhere = pl.BlockSpec(memory_space=pl.ANY)
    return pl.pallas_call(
        functools.partial(kernel, devices, chunks),
        out_shape=(
            jax.ShapeDtypeStruct((CAP, 2, devices, lanes), jnp.float32),
            jax.ShapeDtypeStruct((CAP, devices, lanes), jnp.float32),
        ),
        in_specs=[anywhere, anywhere, vmem, vmem, vmem],
        out_specs=(vmem, vmem),
        scratch_shapes=[
            pltpu.VMEM((chunks, 2, devices * TILE, width), jnp.float32),
            pltpu.VMEM((2, LOOK_ROWS, half), jnp.float32),
            pltpu.VMEM((TILE, devices, half), jnp.float32),
            pltpu.VMEM((TILE, devices, half), jnp.float32),
            pltpu.VMEM((columns, lanes), jnp.bfloat16),
            pltpu.VMEM((quantities * devices, lanes), jnp.float32),
            pltpu.VMEM((total, 3 * BAND * devices), jnp.bfloat16),
            pltpu.VMEM((total, 3 * devices), jnp.bfloat16),
            pltpu.VMEM((total, 3 * devices), jnp.bfloat16),
            pltpu.VMEM((3 * BAND * devices, lanes), jnp.bfloat16),
            pltpu.VMEM((3 * BAND * devices, lanes), jnp.bfloat16),
            pltpu.VMEM((3 * devices, lanes), jnp.bfloat16),
            pltpu.VMEM((total, lanes), jnp.float32),
            pltpu.VMEM((total, lanes), jnp.float32),
            pltpu.SemaphoreType.DMA((chunks, devices)),
            pltpu.SemaphoreType.DMA((chunks, devices)),
            pltpu.SemaphoreType.DMA((chunks,)),
            pltpu.SemaphoreType.DMA((3,)),
            pltpu.SemaphoreType.DMA((devices,)),
            pltpu.SemaphoreType.DMA((devices,)),
        ],
        compiler_params=pltpu.CompilerParams(collective_id=0, has_side_effects=True),
    )(images[0], height_phase, baseline[None], pair_list.T, pair_owner.T)


def solution(mesh):
    in_specs = (
        P(("groups", "date"), None, None, None),
        P(("groups", "date"), None),
        P("groups"),
        P(),
        P(),
    )
    out_specs = (P(("groups", "date"), None, None, None), P(("groups", "date"), None, None))
    return jax.shard_map(body, mesh=mesh, in_specs=in_specs, out_specs=out_specs, check_vma=False)
```

time: 79.4 us -> 50.1 us (0.63)
  Pallas kernels: 0 us -> 46.4 us
  waiting for transfers between devices: 26.9 us -> 0 us
  blocking collectives: 15.2 us -> 0 us
  local copies, waits for them, and re-layouts: 15.9 us -> 2.85 us
  other arithmetic: 10.3 us -> 0 us
  starting transfers between devices: 7.55 us -> 0 us
  matrix products: 2.33 us -> 0 us
    pallas_call x0 -> x1, Pallas kernels: none -> 46.4 us  [body(): pl.pallas_call(functools.partial(kernel, devices, chunks), out_shape=(jax...]
    all_to_all x1 -> x0, waiting for transfers between devices: 26.9 us -> none  [body(): lax.all_to_all(images, 'date', split_axis=2, concat_axis=0, tiled=True)]
    all_to_all x1 -> x0, blocking collectives: 15.2 us -> none  [body(): lax.all_to_all(buffer, 'date', split_axis=0, concat_axis=2, tiled=True)]
    gather x6 -> x0, local copies, waits for them, and re-layouts: 8.45 us -> none  [the longest x1 2.33 us: body(): real_part[second_index]]
    all_to_all x1 -> x0, starting transfers between devices: 7.55 us -> none  [body(): lax.all_to_all(images, 'date', split_axis=2, concat_axis=0, tiled=True)]
    reduce_sum x4 -> x0, other arithmetic: 6.78 us -> none  [the longest x2 6.5 us: multilook(): jnp.sum(values.reshape(values_shape[:-2] + (row_count // LOOK_ROWS, LOOK_...]
    sub x2 -> x0, other arithmetic: 3.43 us -> none  [the longest x1 3.42 us: flatten_phase(): real_part = images[:, 0] * cosine - images[:, 1] * sine_part]
    dot_general x4 -> x0, matrix products: 2.33 us -> none  [the longest x3 2.08 us: multilook(): jnp.dot(flattened, box_matrix(columns), precision=lax.Precision.HIGHEST,...]
  transfers between devices with their start and end apart: 1 -> 0, of which waited for: 1 -> 0; matrix products, arithmetic and copies ran while one was open for 0% -> 0% of each run, Pallas kernels for 0% -> 0%
where the time goes in v1:
time: 50.1 us; the launch traced here: 49.9 us
  Pallas kernels  46.4 us (93%)
  local copies, waits for them, and re-layouts  2.85 us (6%)
  between operations  0.64 us (1%)
    pallas_call x1, Pallas kernels, body(): pl.pallas_call(functools.partial(kernel, devices, chunks), out_shape=(jax...  46.4 us
    unnamed x2, local copies, waits for them, and re-layouts  2.85 us

profile of v1, /device:TPU:0, one launch (start us, length us, event | category | flops | bytes accessed | tf_op | source)
XLA Modules:
  0.0 49.9 jit_solution(474378236829359183)
XLA Ops:
  0.6 46.4 %shard_map.68 = (f32[4,2,16,128]{3,2,1,0:T(8,128)}, f32[4,16,128]{2,1,0:T(8,128)}) custom-call(f32[2,64,2560]{2,1,0:T(8,128)} %bitcast.4, f32[4,2560]{1,0:T(4,128)} %height.1, f32[1,16]{1,0:T(1,128)} %bitcast.6, s32[2,32]{1,0:T(2,128)} %bitcast.5, s32[1,32]{1,0:T(1,128)} %bitcast.7), custom_call_target="tpu_custom_call" | custom-call | tf_op jit(solution)/shard_map/pallas_call | solution.py:280
  47.0 1.5 %copy.9 = f32[4,2,16,128]{3,2,1,0:T(8,128)} copy(f32[4,2,16,128]{3,2,1,0:T(8,128)} %get-tuple-element.4) | data formatting | bytes 131072
  48.5 1.4 %copy.10 = f32[4,16,128]{2,1,0:T(8,128)} copy(f32[4,16,128]{2,1,0:T(8,128)} %get-tuple-element.5) | data formatting | bytes 65536

commit v2 on v0

v2 whole, which is shorter than its diff:
```python
import functools
import math

import jax
import jax.numpy as jnp
from jax import lax
from jax.experimental import pallas as pl
from jax.experimental.pallas import tpu as pltpu
from jax.sharding import PartitionSpec as P

LOOK_ROWS = 4
LOOK_COLS = 20
CAP = 4
BAND = 4
EPSILON = 1e-06
LANES = 128
TILE = 8
LAG = 3


def split(values, parts):
    pieces = []
    for _ in range(parts):
        piece = values.astype(jnp.bfloat16)
        pieces.append(piece)
        values = values - piece.astype(jnp.float32)
    return pieces


def cos_sin(angle):
    square = angle * angle
    sine = jnp.full_like(angle, -1.0 / math.factorial(15))
    for term in range(6, -1, -1):
        sine = sine * square + (-1.0) ** term / math.factorial(2 * term + 1)
    cosine = jnp.full_like(angle, 1.0 / math.factorial(16))
    for term in range(7, -1, -1):
        cosine = cosine * square + (-1.0) ** term / math.factorial(2 * term)
    return cosine, sine * angle


def kernel(
    devices, images, height, baseline, pair_list, pair_owner, looks_out, coherence_out,
    window, heights, box, sums, pick_look, pick_first, pick_second,
    stack_real, stack_imag, stack_power, outbox, inbox,
    plane_send, relay_send, plane_recv, relay_recv, height_send, height_recv, out_send, out_recv,
):
    me = lax.axis_index("date")
    planes = devices // BAND
    plane = lax.div(me, BAND)
    spot = lax.rem(me, BAND)
    rows, columns = images.shape[1:]
    blocks = columns // LANES
    tiles = rows // (2 * BAND * TILE)
    chunks = tiles * blocks
    side = BAND * TILE
    sources = devices // BAND
    look_rows = TILE // LOOK_ROWS

    def peer(step):
        return lax.rem(me + step, devices)

    barrier = pltpu.get_barrier_semaphore()

    @pl.loop(1, devices)
    def _(step):
        pl.semaphore_signal(barrier, inc=1, device_id={"date": peer(step)})

    pl.semaphore_wait(barrier, devices - 1)

    def lines(quarter, upper, chunk):
        first = ((quarter * 2 + upper) * tiles + lax.div(chunk, blocks)) * TILE
        column = lax.rem(chunk, blocks) * LANES
        return images.at[
            :, pl.ds(pl.multiple_of(first, TILE), TILE), pl.ds(pl.multiple_of(column, LANES), LANES)
        ]

    def place(upper, chunk, slot, size=TILE):
        return window.at[upper, chunk, :, pl.ds(pl.multiple_of(slot * TILE, TILE), size), :]

    def own_slot(upper, which):
        return (1 - upper) * BAND + which

    def plane_copy(step, upper, chunk):
        to = spot ^ step
        return pltpu.make_async_remote_copy(
            src_ref=lines(to, upper, chunk),
            dst_ref=place(upper, chunk, own_slot(upper, spot)),
            send_sem=plane_send.at[upper, chunk],
            recv_sem=plane_recv.at[upper, chunk, spot],
            device_id={"date": plane * BAND + to},
        )

    def plane_arrival(step, upper, chunk):
        source = spot ^ step
        return pltpu.make_async_remote_copy(
            src_ref=lines(source, upper, chunk),
            dst_ref=place(upper, chunk, own_slot(upper, source)),
            send_sem=plane_send.at[upper, chunk],
            recv_sem=plane_recv.at[upper, chunk, source],
            device_id={"date": plane * BAND + source},
        )

    def own_copy(upper, chunk):
        return pltpu.make_async_copy(
            lines(spot, upper, chunk),
            place(upper, chunk, own_slot(upper, spot)),
            plane_recv.at[upper, chunk, spot],
        )

    def relays(upper):
        return plane < planes - 1 if upper == 0 else plane > 0

    def gets_relays(upper):
        return plane > 0 if upper == 0 else plane < planes - 1

    def relay_copy(upper, chunk, which, source):
        return pltpu.make_async_remote_copy(
            src_ref=source,
            dst_ref=place(upper, chunk, upper * BAND + which),
            send_sem=relay_send.at[upper, chunk],
            recv_sem=relay_recv.at[upper, chunk],
            device_id={"date": me + BAND * (1 - 2 * upper)},
        )

    def relay_all(upper, chunk):
        return pltpu.make_async_remote_copy(
            src_ref=place(upper, chunk, (1 - upper) * BAND, side),
            dst_ref=place(upper, chunk, upper * BAND, side),
            send_sem=relay_send.at[upper, chunk],
            recv_sem=relay_recv.at[upper, chunk],
            device_id={"date": me},
        )

    def plane_all(upper, chunk):
        return pltpu.make_async_remote_copy(
            src_ref=place(upper, chunk, 0, side - TILE),
            dst_ref=place(upper, chunk, 0, side - TILE),
            send_sem=plane_send.at[upper, chunk],
            recv_sem=relay_recv.at[upper, chunk],
            device_id={"date": me},
        )

    reader = lax.div(me, sources)
    own_height = lax.rem(me, sources)

    def height_copy(to_plane):
        return pltpu.make_async_remote_copy(
            src_ref=height,
            dst_ref=heights.at[own_height],
            send_sem=height_send.at[to_plane],
            recv_sem=height_recv.at[own_height],
            device_id={"date": to_plane * BAND + reader},
        )

    def height_own():
        return pltpu.make_async_copy(height, heights.at[own_height], height_recv.at[own_height])

    def height_arrival(source):
        return pltpu.make_async_remote_copy(
            src_ref=height,
            dst_ref=heights.at[source],
            send_sem=height_send.at[0],
            recv_sem=height_recv.at[source],
            device_id={"date": me},
        )

    @pl.loop(0, planes)
    def _(to_plane):
        @pl.when(to_plane * BAND + reader != me)
        def _():
            height_copy(to_plane).start()

        @pl.when(to_plane * BAND + reader == me)
        def _():
            height_own().start()

    @pl.loop(0, chunks)
    def _(chunk):
        for upper in range(2):
            for step in (2, 3, 1):
                plane_copy(step, upper, chunk).start()

            @pl.when(relays(upper))
            def _():
                relay_copy(upper, chunk, spot, lines(spot, upper, chunk)).start()

            own_copy(upper, chunk).start()

    for upper in range(2):
        @pl.when(jnp.logical_not(gets_relays(upper)))
        def _():
            @pl.loop(0, chunks)
            def _(chunk):
                window[upper, chunk, :, upper * side:(upper + 1) * side, :] = jnp.zeros(
                    (2, side, LANES), jnp.float32
                )

    position = lax.broadcasted_iota(jnp.int32, (columns, LANES), 0)
    target = lax.broadcasted_iota(jnp.int32, (columns, LANES), 1) * LOOK_COLS
    box[...] = jnp.where(
        (position >= target) & (position < target + LOOK_COLS), 1.0, 0.0
    ).astype(jnp.bfloat16)
    sums[...] = jnp.zeros_like(sums)

    dates = 2 * BAND
    lane = lax.broadcasted_iota(jnp.int32, (dates, devices), 1)
    date = lax.broadcasted_iota(jnp.int32, (dates, devices), 0)
    scales = []
    for upper in range(2):
        chosen_date = lane == date + (plane - 1 + upper) * BAND
        scales.append(
            jnp.sum(jnp.where(chosen_date, baseline[...], 0.0), axis=1, keepdims=True)
        )

    owner = pair_owner[...].astype(jnp.float32)
    pairs = owner.shape[1]
    down = lax.broadcasted_iota(jnp.int32, (pairs, pairs), 0)
    across = lax.broadcasted_iota(jnp.int32, (pairs, pairs), 1)
    owner_column = jnp.sum(jnp.where(down == across, owner, 0.0), axis=1, keepdims=True)
    earlier = (owner_column == owner) & (down < across)
    spot_of = owner * TILE + jnp.sum(jnp.where(earlier, 1.0, 0.0), axis=0, keepdims=True)
    first = pair_list[0:1, :]
    second = pair_list[1:2, :]
    total = devices * TILE
    line = lax.broadcasted_iota(jnp.int32, (total, pairs), 0)
    taken = (line - (line & CAP)).astype(jnp.float32) == spot_of

    def pick(value, valid, size):
        lane = lax.broadcasted_iota(jnp.int32, (total, 3 * size), 1) & (size - 1)
        listed = jnp.sum(
            jnp.where(taken & valid, value.astype(jnp.float32) + 1.0, 0.0), axis=1, keepdims=True
        ) - 1.0
        return jnp.where(lane.astype(jnp.float32) == listed, 1.0, 0.0).astype(jnp.bfloat16)

    for upper in range(2):
        ends_here = second if upper == 0 else first
        valid = (ends_here >= plane * BAND) & (ends_here < (plane + 1) * BAND)
        start = first - (plane - 1 + upper) * BAND
        distance = second - first
        pick_look[upper] = pick((distance - 1) * dates + start, valid, BAND * dates)
        pick_first[upper] = pick(start, valid, dates)
        pick_second[upper] = pick(start + distance, valid, dates)

    @pl.loop(0, sources)
    def _(source):
        height_arrival(source).wait_recv()

    def forward(chunk):
        for upper in range(2):
            own_copy(upper, chunk).wait()
        for step in (1, 2, 3):
            for upper in range(2):
                plane_arrival(step, upper, chunk).wait_recv()

                @pl.when(relays(upper))
                def _():
                    which = spot ^ step
                    relay_copy(
                        upper, chunk, which, place(upper, chunk, own_slot(upper, which))
                    ).start()

    def compute(chunk):
        for upper in range(2):
            @pl.when(gets_relays(upper))
            def _():
                relay_all(upper, chunk).wait_recv()

        tile = lax.div(chunk, blocks)
        column = pl.multiple_of(lax.rem(chunk, blocks) * LANES, LANES)
        totals = []
        for upper in range(2):
            for look_row in range(look_rows):
                found = [None] * (1 + 2 * BAND)

                def add(at, value):
                    found[at] = value if found[at] is None else found[at] + value

                source = (upper * tiles + tile) * look_rows + look_row
                for row in range(LOOK_ROWS):
                    level = heights[source, row:row + 1, pl.ds(column, LANES)]
                    cosine, sine = cos_sin(scales[upper] * level)
                    at = pl.ds(look_row * LOOK_ROWS + row, dates, stride=TILE)
                    real = window[upper, chunk, 0, at, :]
                    imag = window[upper, chunk, 1, at, :]
                    flat_real = real * cosine - imag * sine
                    flat_imag = real * sine + imag * cosine
                    add(0, flat_real * flat_real + flat_imag * flat_imag)
                    for distance in range(1, BAND + 1):
                        next_real = pltpu.roll(flat_real, dates - distance, 0)
                        next_imag = pltpu.roll(flat_imag, dates - distance, 0)
                        add(distance, flat_real * next_real + flat_imag * next_imag)
                        add(BAND + distance, flat_imag * next_real - flat_real * next_imag)
                totals.extend(found)
        weights = box[pl.ds(column, LANES), :]
        summed = sums[tile]
        for piece in split(jnp.concatenate(totals, axis=0), 2):
            summed = summed + jnp.dot(piece, weights, preferred_element_type=jnp.float32)
        sums[tile] = summed

    @pl.loop(0, LAG)
    def _(chunk):
        forward(chunk)

    @pl.loop(LAG, chunks)
    def _(chunk):
        forward(chunk)
        compute(chunk - LAG)

    @pl.loop(chunks - LAG, chunks)
    def _(chunk):
        compute(chunk)

    def chosen(pick_matrix, stack):
        return jnp.dot(pick_matrix, stack[...], preferred_element_type=jnp.float32)

    kind = lax.broadcasted_iota(jnp.int32, (total, LANES), 0) & CAP
    quantities = (1 + 2 * BAND) * dates
    ends = (0, dates, (1 + BAND) * dates, quantities)
    for tile in range(tiles):
        mean = sums[tile] * (1.0 / (LOOK_ROWS * LOOK_COLS))
        for upper in range(2):
            ratios = []
            for look_row in range(look_rows):
                base = (upper * look_rows + look_row) * quantities
                for stack, low, high in zip((stack_power, stack_real, stack_imag), ends[:-1], ends[1:]):
                    size = high - low
                    stack[...] = jnp.concatenate(
                        [p.astype(jnp.float32) for p in split(mean[base + low:base + high], 3)], axis=0
                    ).astype(jnp.bfloat16)
                look_real = chosen(pick_look[upper], stack_real)
                look_imag = chosen(pick_look[upper], stack_imag)
                denominator = jnp.sqrt(
                    (chosen(pick_first[upper], stack_power) + EPSILON)
                    * (chosen(pick_second[upper], stack_power) + EPSILON)
                )
                ratios.append(jnp.sqrt(look_real * look_real + look_imag * look_imag) / denominator)
                outbox[(tile * 2 + upper) * 3 + look_row] = jnp.where(kind == 0, look_real, look_imag)
            outbox[(tile * 2 + upper) * 3 + 2] = jnp.where(kind == 0, ratios[0], ratios[1])

    def parcel(which):
        return pl.ds(pl.multiple_of(which * TILE, TILE), TILE)

    def out_copy(to):
        return pltpu.make_async_remote_copy(
            src_ref=outbox.at[:, parcel(to), :],
            dst_ref=inbox.at[me],
            send_sem=out_send.at[to],
            recv_sem=out_recv.at[me],
            device_id={"date": to},
        )

    def out_arrival(source):
        return pltpu.make_async_remote_copy(
            src_ref=outbox.at[:, parcel(source), :],
            dst_ref=inbox.at[source],
            send_sem=out_send.at[source],
            recv_sem=out_recv.at[source],
            device_id={"date": source},
        )

    @pl.loop(1, devices)
    def _(step):
        out_copy(peer(step)).start()

    inbox[me] = outbox[:, parcel(me), :]

    @pl.loop(0, planes)
    def _(to_plane):
        @pl.when(to_plane * BAND + reader != me)
        def _():
            height_copy(to_plane).wait_send()

    @pl.loop(0, chunks)
    def _(chunk):
        for upper in range(2):
            plane_all(upper, chunk).wait_send()

            @pl.when(relays(upper))
            def _():
                relay_all(upper, chunk).wait_send()

    @pl.loop(1, devices)
    def _(step):
        out_arrival(peer(step)).wait_recv()

    height_rows = 2 * tiles * look_rows * BAND
    for quarter in range(BAND):
        for tile in range(tiles):
            for upper in range(2):
                for part in range(3):
                    value = inbox[quarter, (tile * 2 + upper) * 3 + part]
                    for other in range(1, planes):
                        value = value + inbox[other * BAND + quarter, (tile * 2 + upper) * 3 + part]
                    row = ((quarter * 2 + upper) * tiles + tile) * look_rows
                    for c in range(2):
                        piece = value[c * CAP:(c + 1) * CAP]
                        if part < 2:
                            looks_out[pl.ds(c * height_rows + row + part, CAP, stride=2 * height_rows), :] = piece
                        else:
                            coherence_out[pl.ds(row + c, CAP, stride=height_rows), :] = piece

    @pl.loop(1, devices)
    def _(step):
        out_copy(peer(step)).wait_send()


def body(images, height_phase, baseline, pair_list, pair_owner):
    devices = lax.axis_size("date")
    rows, columns = images.shape[2:]
    lanes = columns // LOOK_COLS
    looks = rows // LOOK_ROWS
    tiles = rows // (2 * BAND * TILE)
    chunks = tiles * (columns // LANES)
    dates = 2 * BAND
    assert lanes == LANES and rows == LOOK_ROWS * devices and TILE == 2 * LOOK_ROWS
    assert rows % (2 * BAND * TILE) == 0 and columns % LANES == 0
    quantities = 1 + 2 * BAND
    total = devices * TILE
    vmem = pl.BlockSpec(memory_space=pltpu.VMEM)
    hbm = pl.BlockSpec(memory_space=pltpu.HBM)
    look, coherence = pl.pallas_call(
        functools.partial(kernel, devices),
        out_shape=(
            jax.ShapeDtypeStruct((CAP * 2 * looks, lanes), jnp.float32),
            jax.ShapeDtypeStruct((CAP * looks, lanes), jnp.float32),
        ),
        in_specs=[hbm, hbm, vmem, vmem, vmem],
        out_specs=(vmem, vmem),
        scratch_shapes=[
            pltpu.VMEM((2, chunks, 2, dates * TILE, LANES), jnp.float32),
            pltpu.VMEM((devices // BAND, LOOK_ROWS, columns), jnp.float32),
            pltpu.VMEM((columns, lanes), jnp.bfloat16),
            pltpu.VMEM((tiles, 4 * quantities * dates, lanes), jnp.float32),
            pltpu.VMEM((2, total, 3 * BAND * dates), jnp.bfloat16),
            pltpu.VMEM((2, total, 3 * dates), jnp.bfloat16),
            pltpu.VMEM((2, total, 3 * dates), jnp.bfloat16),
            pltpu.VMEM((3 * BAND * dates, lanes), jnp.bfloat16),
            pltpu.VMEM((3 * BAND * dates, lanes), jnp.bfloat16),
            pltpu.VMEM((3 * dates, lanes), jnp.bfloat16),
            pltpu.VMEM((tiles * 6, total, lanes), jnp.float32),
            pltpu.VMEM((devices, tiles * 6, TILE, lanes), jnp.float32),
            pltpu.SemaphoreType.DMA((2, chunks)),
            pltpu.SemaphoreType.DMA((2, chunks)),
            pltpu.SemaphoreType.DMA((2, chunks, BAND)),
            pltpu.SemaphoreType.DMA((2, chunks)),
            pltpu.SemaphoreType.DMA((devices // BAND,)),
            pltpu.SemaphoreType.DMA((devices // BAND,)),
            pltpu.SemaphoreType.DMA((devices,)),
            pltpu.SemaphoreType.DMA((devices,)),
        ],
        compiler_params=pltpu.CompilerParams(
            collective_id=0, has_side_effects=True, vmem_limit_bytes=44 << 20
        ),
    )(images[0], height_phase, baseline[None], pair_list.T, pair_owner.T)
    return look.reshape(CAP, 2, looks, lanes), coherence.reshape(CAP, looks, lanes)


def solution(mesh):
    in_specs = (
        P(("groups", "date"), None, None, None),
        P(("groups", "date"), None),
        P("groups"),
        P(),
        P(),
    )
    out_specs = (P(("groups", "date"), None, None, None), P(("groups", "date"), None, None))
    return jax.shard_map(body, mesh=mesh, in_specs=in_specs, out_specs=out_specs, check_vma=False)
```

time: 79.4 us -> 46.6 us (0.59)
  Pallas kernels: 0 us -> 40.3 us
  waiting for transfers between devices: 26.9 us -> 0 us
  blocking collectives: 15.2 us -> 0 us
  local copies, waits for them, and re-layouts: 15.9 us -> 5.32 us
  other arithmetic: 10.3 us -> 0 us
  starting transfers between devices: 7.55 us -> 0 us
  matrix products: 2.33 us -> 0 us
    pallas_call x0 -> x1, Pallas kernels: none -> 40.3 us  [body(): pl.pallas_call(functools.partial(kernel, devices), out_shape=(jax.ShapeDt...]
    all_to_all x1 -> x0, waiting for transfers between devices: 26.9 us -> none  [body(): lax.all_to_all(images, 'date', split_axis=2, concat_axis=0, tiled=True)]
    all_to_all x1 -> x0, blocking collectives: 15.2 us -> none  [body(): lax.all_to_all(buffer, 'date', split_axis=0, concat_axis=2, tiled=True)]
    gather x6 -> x0, local copies, waits for them, and re-layouts: 8.45 us -> none  [the longest x1 2.33 us: body(): real_part[second_index]]
    all_to_all x1 -> x0, starting transfers between devices: 7.55 us -> none  [body(): lax.all_to_all(images, 'date', split_axis=2, concat_axis=0, tiled=True)]
    reduce_sum x4 -> x0, other arithmetic: 6.78 us -> none  [the longest x2 6.5 us: multilook(): jnp.sum(values.reshape(values_shape[:-2] + (row_count // LOOK_ROWS, LOOK_...]
    sub x2 -> x0, other arithmetic: 3.43 us -> none  [the longest x1 3.42 us: flatten_phase(): real_part = images[:, 0] * cosine - images[:, 1] * sine_part]
    dot_general x4 -> x0, matrix products: 2.33 us -> none  [the longest x3 2.08 us: multilook(): jnp.dot(flattened, box_matrix(columns), precision=lax.Precision.HIGHEST,...]
  transfers between devices with their start and end apart: 1 -> 0, of which waited for: 1 -> 0; matrix products, arithmetic and copies ran while one was open for 0% -> 0% of each run, Pallas kernels for 0% -> 0%
where the time goes in v2:
time: 46.6 us; the launch traced here: 46.3 us
  Pallas kernels  40.3 us (86%)
  local copies, waits for them, and re-layouts  5.32 us (11%)
  between operations  0.65 us (1%)
    pallas_call x1, Pallas kernels, body(): pl.pallas_call(functools.partial(kernel, devices), out_shape=(jax.ShapeDt...  40.3 us
    unnamed x12, local copies, waits for them, and re-layouts  5.32 us

profile of v2, /device:TPU:0, one launch (start us, length us, event | category | flops | bytes accessed | tf_op | source)
XLA Modules:
  0.0 46.3 jit_solution(10753985894866926737)
XLA Ops:
  0.6 0.0 copy-start
  0.6 1.3 %copy-done = f32[1,2,64,2560]{3,2,1,0:T(8,128)S(1)} copy-done((f32[1,2,64,2560]{3,2,1,0:T(8,128)S(1)}, f32[1,2,64,2560]{3,2,1,0:T(8,128)}, u32[]{:S(2)}) %copy-start) | copy-done | bytes 1310744
  1.9 0.0 copy-start.1
  2.0 0.8 %copy-done.1 = f32[4,2560]{1,0:T(4,128)S(1)} copy-done((f32[4,2560]{1,0:T(4,128)S(1)}, f32[4,2560]{1,0:T(4,128)}, u32[]{:S(2)}) %copy-start.1) | copy-done | bytes 40984
  2.7 0.0 copy-start.2
  2.7 0.7 %copy-done.2 = s32[32,2]{0,1:T(2,128)S(1)} copy-done((s32[32,2]{0,1:T(2,128)S(1)}, s32[32,2]{0,1:T(2,128)}, u32[]{:S(2)}) %copy-start.2) | copy-done | bytes 280
  3.4 0.0 copy-start.3
  3.4 0.7 %copy-done.3 = f32[16]{0:T(128)S(1)} copy-done((f32[16]{0:T(128)S(1)}, f32[16]{0:T(128)}, u32[]{:S(2)}) %copy-start.3) | copy-done | bytes 88
  4.1 0.0 copy-start.4
  4.1 0.7 %copy-done.4 = s32[32,1]{0,1:T(1,128)S(1)} copy-done((s32[32,1]{0,1:T(1,128)S(1)}, s32[32,1]{0,1:T(1,128)}, u32[]{:S(2)}) %copy-start.4) | copy-done | bytes 152
  4.7 40.3 %shard_map.68 = (f32[128,128]{1,0:T(8,128)S(1)}, f32[64,128]{1,0:T(8,128)S(1)}) custom-call(f32[2,64,2560]{2,1,0:T(8,128)S(1)} %bitcast.6, f32[4,2560]{1,0:T(4,128)S(1)} %copy-done.1, f32[1,16]{1,0:T(1,128)S(1)} %bitcast.10, s32[2,32]{1,0:T(2,128)S(1)} %bitcast.9, s32[1,32]{1,0:T(1,128)S(1)} %bitcast.11), custom_call_target="tpu_custom_call" | custom-call | tf_op jit(solution)/shard_map/pallas_call | solution.py:421
  45.1 0.6 %copy.9 = f32[4,2,16,128]{3,2,1,0:T(8,128)} copy(f32[4,2,16,128]{3,2,1,0:T(8,128)S(1)} %bitcast.7) | data formatting | bytes 131072
  45.7 0.6 %copy.10 = f32[4,16,128]{2,1,0:T(8,128)} copy(f32[4,16,128]{2,1,0:T(8,128)S(1)} %bitcast.8) | data formatting | bytes 65536
Async XLA Ops:
  0.6 1.3 %copy-start = (f32[1,2,64,2560]{3,2,1,0:T(8,128)S(1)}, f32[1,2,64,2560]{3,2,1,0:T(8,128)}, u32[]{:S(2)}) copy-start(f32[1,2,64,2560]{3,2,1,0:T(8,128)} %param.5) | copy-start | bytes 3932164
  1.9 0.8 %copy-start.1 = (f32[4,2560]{1,0:T(4,128)S(1)}, f32[4,2560]{1,0:T(4,128)}, u32[]{:S(2)}) copy-start(f32[4,2560]{1,0:T(4,128)} %height.1) | copy-start | bytes 122884
  2.7 0.7 %copy-start.2 = (s32[32,2]{0,1:T(2,128)S(1)}, s32[32,2]{0,1:T(2,128)}, u32[]{:S(2)}) copy-start(s32[32,2]{0,1:T(2,128)} %param.8) | copy-start | bytes 772
  3.4 0.7 %copy-start.3 = (f32[16]{0:T(128)S(1)}, f32[16]{0:T(128)}, u32[]{:S(2)}) copy-start(f32[16]{0:T(128)} %param.7) | copy-start | bytes 196
  4.1 0.7 %copy-start.4 = (s32[32,1]{0,1:T(1,128)S(1)}, s32[32,1]{0,1:T(1,128)}, u32[]{:S(2)}) copy-start(s32[32,1]{0,1:T(1,128)} %param.9) | copy-start | bytes 388

commit v3 on v2

--- a/solution.py
+++ b/solution.py
@@ -15,7 +15,8 @@
 EPSILON = 1e-06
 LANES = 128
 TILE = 8
-LAG = 3
+LAG = 5
+AHEAD = 8
 
 
 def split(values, parts):
@@ -240,10 +241,6 @@
         pick_look[upper] = pick((distance - 1) * dates + start, valid, BAND * dates)
         pick_first[upper] = pick(start, valid, dates)
         pick_second[upper] = pick(start + distance, valid, dates)
-
-    @pl.loop(0, sources)
-    def _(source):
-        height_arrival(source).wait_recv()
 
     def forward(chunk):
         for upper in range(2):
@@ -297,11 +294,19 @@
             summed = summed + jnp.dot(piece, weights, preferred_element_type=jnp.float32)
         sums[tile] = summed
 
-    @pl.loop(0, LAG)
+    @pl.loop(0, AHEAD)
     def _(chunk):
         forward(chunk)
 
-    @pl.loop(LAG, chunks)
+    @pl.loop(0, sources)
+    def _(source):
+        height_arrival(source).wait_recv()
+
+    @pl.loop(0, AHEAD - LAG)
+    def _(chunk):
+        compute(chunk)
+
+    @pl.loop(AHEAD, chunks)
     def _(chunk):
         forward(chunk)
         compute(chunk - LAG)
@@ -449,7 +454,7 @@
             pltpu.SemaphoreType.DMA((devices,)),
         ],
         compiler_params=pltpu.CompilerParams(
-            collective_id=0, has_side_effects=True, vmem_limit_bytes=44 << 20
+            collective_id=0, has_side_effects=True
         ),
     )(images[0], height_phase, baseline[None], pair_list.T, pair_owner.T)
     return look.reshape(CAP, 2, looks, lanes), coherence.reshape(CAP, looks, lanes)

time: 46.6 us -> 42.9 us (0.921)
  the two profiles are of different devices: /device:TPU:0 before, /device:TPU:13 now
where the time goes in v3:
time: 42.9 us; the launch traced here: 42.7 us
  Pallas kernels  39.2 us (91%)
  local copies, waits for them, and re-layouts  2.85 us (7%)
  between operations  0.64 us (1%)
    pallas_call x1, Pallas kernels, body(): pl.pallas_call(functools.partial(kernel, devices), out_shape=(jax.ShapeDt...  39.2 us
    unnamed x2, local copies, waits for them, and re-layouts  2.85 us

profile of v3, /device:TPU:13, one launch (start us, length us, event | category | flops | bytes accessed | tf_op | source)
XLA Modules:
  0.0 42.7 jit_solution(11864283690490009236)
XLA Ops:
  0.6 39.2 %shard_map.68 = (f32[128,128]{1,0:T(8,128)}, f32[64,128]{1,0:T(8,128)}) custom-call(f32[2,64,2560]{2,1,0:T(8,128)} %bitcast.6, f32[4,2560]{1,0:T(4,128)} %height.1, f32[1,16]{1,0:T(1,128)} %bitcast.10, s32[2,32]{1,0:T(2,128)} %bitcast.9, s32[1,32]{1,0:T(1,128)} %bitcast.11), custom_call_target="tpu_custom_call" | custom-call | tf_op jit(solution)/shard_map/pallas_call | solution.py:426
  39.8 1.5 %copy.9 = f32[4,2,16,128]{3,2,1,0:T(8,128)} copy(f32[4,2,16,128]{3,2,1,0:T(8,128)} %bitcast.7) | data formatting | bytes 131072
  41.3 1.4 %copy.10 = f32[4,16,128]{2,1,0:T(8,128)} copy(f32[4,16,128]{2,1,0:T(8,128)} %bitcast.8) | data formatting | bytes 65536
